TPU v7x, 32 devices: a whole 2x2x4 slice. The times are simulated.
32 devices in a mesh: dp: 8 (over z, y), tensor: 4 (over x, core).
Axes of the slice: x: 2, y: 2, z: 4, core: 2. Of those that a mesh axis runs over, the one named last changes fastest.
Arguments:
- tokens: bfloat16 [16, 2048, 768], P('dp', 'tensor'), may hold values from -6 to 6
- segment_ids: int32 [16, 2048], P('dp'), may hold values from 0 to 11, never falling along the last dimension, each value on 1 to 1024 neighbouring positions
- w_query: bfloat16 [768, 768], P('dp', 'tensor'), may hold values from -0.21875 to 0.21875
- w_key: bfloat16 [768, 768], P('dp', 'tensor'), may hold values from -0.21875 to 0.21875
- w_value: bfloat16 [768, 768], P('dp', 'tensor'), may hold values from -0.21875 to 0.21875
- w_out: bfloat16 [768, 768], P('tensor', 'dp'), may hold values from -1.25 to 1.25
- b_query: bfloat16 [12, 64], P('tensor', 'dp'), may hold values from -3 to 3
- b_value: bfloat16 [12, 64], P('tensor', 'dp'), may hold values from -3 to 3
- w_up: bfloat16 [768, 3072], P('dp', 'tensor'), may hold values from -0.21875 to 0.21875
- w_down: bfloat16 [3072, 768], P('tensor', 'dp'), may hold values from -0.109375 to 0.109375
- b_up: bfloat16 [48, 64], P('tensor', 'dp'), may hold values from -3 to 3
- b_out: bfloat16 [768], P(('dp', 'tensor')), may hold values from -3 to 3
- gain_one: bfloat16 [768], P(('dp', 'tensor')), may hold values from 0.25 to 1.75
- shift_one: bfloat16 [768], P(('dp', 'tensor')), may hold values from -3 to 3
- b_down: bfloat16 [768], P(('dp', 'tensor')), may hold values from -3 to 3
- gain_two: bfloat16 [768], P(('dp', 'tensor')), may hold values from 0.25 to 1.75
- shift_two: bfloat16 [768], P(('dp', 'tensor')), may hold values from -3 to 3
- cotangent: float32 [16, 2048, 768], P('dp', 'tensor'), may hold values from -6 to 6
Outputs:
- layer_out: float32 [16, 2048, 768], P('dp', 'tensor')
- grad_tokens: float32 [16, 2048, 768], P('dp', 'tensor')
- grad_w_query: float32 [768, 768], P('dp', 'tensor')
- grad_w_key: float32 [768, 768], P('dp', 'tensor')
- grad_w_value: float32 [768, 768], P('dp', 'tensor')
- grad_w_out: float32 [768, 768], P('tensor', 'dp')
- grad_b_query: float32 [12, 64], P('tensor', 'dp')
- grad_b_value: float32 [12, 64], P('tensor', 'dp')
- grad_w_up: float32 [768, 3072], P('dp', 'tensor')
- grad_w_down: float32 [3072, 768], P('tensor', 'dp')
- grad_b_up: float32 [48, 64], P('tensor', 'dp')
- grad_b_out: float32 [768], P(('dp', 'tensor'))
- grad_gain_one: float32 [768], P(('dp', 'tensor'))
- grad_shift_one: float32 [768], P(('dp', 'tensor'))
- grad_b_down: float32 [768], P(('dp', 'tensor'))
- grad_gain_two: float32 [768], P(('dp', 'tensor'))
- grad_shift_two: float32 [768], P(('dp', 'tensor'))
Inputs may be any that keep to these rules, and one draw needn't show every extreme that they name: `segment_ids`: in each sequence the segment numbers never fall and each of the 12 segments spans 1 to 1024 positions; some segment spans exactly 1024.
All inputs are finite; a program needn't handle non-finite values.
Results may differ from a plain program's by a relative error of at most 0.015.
Values may be sent and summed in bfloat16 or wider, within the bound.
No kernel may reach another device: no remote copies, remote signals or barrier semaphores. Data moves between devices by JAX's collectives and lax.ppermute only.
A program may use at most 192 MiB of HBM per device.

v0:
```python
import jax
import jax.numpy as jnp
from jax import lax
from jax.sharding import PartitionSpec as P

HD = 64
epsilon = 1e-12


def normalize(summed, gain, shift):
    centre = jnp.mean(summed, axis=-1, keepdims=True)
    centred = summed - centre
    spread = jnp.mean(centred * centred, axis=-1, keepdims=True)
    return centred * lax.rsqrt(spread + epsilon) * gain + shift


def gelu_exact(v):
    return jax.nn.gelu(v, approximate=False)


def block_scores(query_rows, key_heads, query_segs, key_segs, scale):
    scores = (
        jnp.einsum("qhd,khd->hqk", query_rows, key_heads, preferred_element_type=jnp.float32)
        * scale
    )
    same_doc = query_segs[:, None] == key_segs[None, :]
    return jnp.where(same_doc[None, :, :], scores, -1e30)


def attention_forward(queries, key_heads, value_heads, segments, block, scale):
    sequences, length = segments.shape
    blocks = length // block

    def one_block(index):
        which = index // blocks
        start = index % blocks * block
        query_rows = lax.dynamic_slice_in_dim(queries[which], start, block, 0)
        query_segs = lax.dynamic_slice_in_dim(segments[which], start, block, 0)
        scores = block_scores(query_rows, key_heads[which], query_segs, segments[which], scale)
        summit = jnp.max(scores, axis=-1, keepdims=True)
        raised = jnp.exp(scores - summit)
        totals = jnp.sum(raised, axis=-1, keepdims=True)
        weights = (raised / totals).astype(jnp.bfloat16)
        output = jnp.einsum(
            "hqk,khd->qhd", weights, value_heads[which], preferred_element_type=jnp.float32
        )
        return (output.astype(jnp.bfloat16), (summit + jnp.log(totals))[:, :, 0])

    outputs, logsums = lax.map(one_block, jnp.arange(sequences * blocks, dtype=jnp.int32))
    heads = queries.shape[2]
    context = outputs.reshape(sequences, length, heads, queries.shape[3])
    return (context, logsums.reshape(sequences, blocks, heads, block))


def attention_backward(
    queries, key_heads, value_heads, segments, logsums, grad_context, block, scale
):
    sequences, length = segments.shape
    blocks = length // block
    heads = queries.shape[2]
    head_size = queries.shape[3]

    def one_sequence(which):
        keys_here = key_heads[which]
        values_here = value_heads[which]
        segs_here = segments[which]

        def one_step(carry, position):
            gradient_key_rows, gradient_value_rows = carry
            start = position * block
            query_rows = lax.dynamic_slice_in_dim(queries[which], start, block, 0)
            grad_rows = lax.dynamic_slice_in_dim(grad_context[which], start, block, 0)
            query_segs = lax.dynamic_slice_in_dim(segs_here, start, block, 0)
            scores = block_scores(query_rows, keys_here, query_segs, segs_here, scale)
            weights = jnp.exp(scores - logsums[which, position][:, :, None])
            grad_weights = jnp.einsum(
                "qhd,khd->hqk", grad_rows, values_here, preferred_element_type=jnp.float32
            )
            inner_sum = jnp.sum(weights * grad_weights, axis=-1, keepdims=True)
            grad_scores = (weights * (grad_weights - inner_sum)).astype(jnp.bfloat16)
            grad_query = (
                jnp.einsum(
                    "hqk,khd->qhd", grad_scores, keys_here, preferred_element_type=jnp.float32
                )
                * scale
            )
            gradient_key_rows = (
                gradient_key_rows
                + jnp.einsum(
                    "hqk,qhd->khd", grad_scores, query_rows, preferred_element_type=jnp.float32
                )
                * scale
            )
            gradient_value_rows = gradient_value_rows + jnp.einsum(
                "hqk,qhd->khd",
                weights.astype(jnp.bfloat16),
                grad_rows,
                preferred_element_type=jnp.float32,
            )
            return ((gradient_key_rows, gradient_value_rows), grad_query.astype(jnp.bfloat16))

        zeros = jnp.zeros((length, heads, head_size), jnp.float32)
        (gradient_key_rows, gradient_value_rows), gradient_query_rows = lax.scan(
            one_step, (zeros, zeros), jnp.arange(blocks, dtype=jnp.int32)
        )
        return (
            gradient_query_rows.reshape(length, heads, head_size),
            gradient_key_rows.astype(jnp.bfloat16),
            gradient_value_rows.astype(jnp.bfloat16),
        )

    return lax.map(one_sequence, jnp.arange(sequences, dtype=jnp.int32))


def per_device(
    tokens,
    segment_ids,
    w_query,
    w_key,
    w_value,
    w_out,
    b_query,
    b_value,
    w_up,
    w_down,
    b_up,
    b_out,
    gain_one,
    shift_one,
    b_down,
    gain_two,
    shift_two,
    cotangent,
):
    (
        query_columns,
        key_columns,
        value_columns,
        output_rows,
        query_bias,
        value_bias,
        up_cols,
        down_rows,
        up_bias,
    ) = (
        lax.all_gather(w_query, "dp", axis=0, tiled=True),
        lax.all_gather(w_key, "dp", axis=0, tiled=True),
        lax.all_gather(w_value, "dp", axis=0, tiled=True),
        lax.all_gather(w_out, "dp", axis=1, tiled=True),
        lax.all_gather(b_query, "dp", axis=1, tiled=True),
        lax.all_gather(b_value, "dp", axis=1, tiled=True),
        lax.all_gather(w_up, "dp", axis=0, tiled=True),
        lax.all_gather(w_down, "dp", axis=1, tiled=True),
        lax.all_gather(b_up, "dp", axis=1, tiled=True),
    )
    vectors = (
        lax.all_gather(b_out, ("dp", "tensor"), axis=0, tiled=True),
        lax.all_gather(gain_one, ("dp", "tensor"), axis=0, tiled=True),
        lax.all_gather(shift_one, ("dp", "tensor"), axis=0, tiled=True),
        lax.all_gather(b_down, ("dp", "tensor"), axis=0, tiled=True),
        lax.all_gather(gain_two, ("dp", "tensor"), axis=0, tiled=True),
        lax.all_gather(shift_two, ("dp", "tensor"), axis=0, tiled=True),
    )
    out_bias, first_gain, first_shift, down_bias, second_gain, second_shift = [
        v.astype(jnp.float32) for v in vectors
    ]
    collected_rows = lax.all_gather(tokens, "tensor", axis=1, tiled=True)
    sequences, length, features = collected_rows.shape
    heads = query_columns.shape[1] // HD
    scale = HD ** (-0.5)
    block = min(512, length)

    def heads_of(weight_matrix, bias_vector):
        product = (
            jnp.einsum(
                "nfu,ua->nfa", collected_rows, weight_matrix, preferred_element_type=jnp.float32
            )
            + bias_vector
        )
        return product.astype(jnp.bfloat16).reshape(sequences, length, heads, HD)

    queries = heads_of(query_columns, query_bias.reshape(-1).astype(jnp.float32))
    key_heads = heads_of(key_columns, 0.0)
    value_heads = heads_of(value_columns, value_bias.reshape(-1).astype(jnp.float32))
    context, logsums = attention_forward(queries, key_heads, value_heads, segment_ids, block, scale)
    context_merged = context.reshape(sequences, length, heads * HD)
    partial_out = jnp.einsum(
        "zta,ag->ztg", context_merged, output_rows, preferred_element_type=jnp.float32
    )
    attended = lax.psum_scatter(partial_out, "tensor", scatter_dimension=1, tiled=True)
    summed = tokens.astype(jnp.float32) + attended + out_bias
    normed, first_pull = jax.vjp(normalize, summed, first_gain, first_shift)
    normed_low = normed.astype(jnp.bfloat16)
    normalized_total = lax.all_gather(normed_low, "tensor", axis=1, tiled=True)
    up_weight_used, down_weight_used, upbias_use = (up_cols, down_rows, up_bias)
    hidden_input = jnp.einsum(
        "uah,hg->uag", normalized_total, up_weight_used, preferred_element_type=jnp.float32
    )
    hidden_input = hidden_input + upbias_use.reshape(-1).astype(jnp.float32)
    activated, gelu_pull = jax.vjp(gelu_exact, hidden_input)
    activated_reduced = activated.astype(jnp.bfloat16)
    branch_part = jnp.einsum(
        "xvt,tw->xvw", activated_reduced, down_weight_used, preferred_element_type=jnp.float32
    )
    branch = lax.psum_scatter(branch_part, "tensor", scatter_dimension=1, tiled=True)
    layer_out, second_pull = jax.vjp(
        normalize, normed + branch + down_bias, second_gain, second_shift
    )
    grad_sum_two, grad_gain_two, grad_shift_two = second_pull(cotangent)
    grad_down_bias = jnp.sum(grad_sum_two, axis=(0, 1))
    grad_branch = grad_sum_two.astype(jnp.bfloat16)
    gradient_branch_total = lax.all_gather(grad_branch, "tensor", axis=1, tiled=True)
    grad_down = jnp.einsum(
        "ypw,ypv->wv", activated_reduced, gradient_branch_total, preferred_element_type=jnp.float32
    )
    grad_act = jnp.einsum(
        "mti,oi->mto", gradient_branch_total, down_weight_used, preferred_element_type=jnp.float32
    )
    gradient_hidden = gelu_pull(grad_act)[0].astype(jnp.bfloat16)
    grad_up_bias = jnp.sum(gradient_hidden, axis=(0, 1), dtype=jnp.float32).reshape(-1, HD)
    gradient_up_weight = jnp.einsum(
        "qwc,qwb->cb", normalized_total, gradient_hidden, preferred_element_type=jnp.float32
    )
    backward_portion = jnp.einsum(
        "hez,bz->heb", gradient_hidden, up_weight_used, preferred_element_type=jnp.float32
    )
    grad_normed = grad_sum_two + lax.psum_scatter(
        backward_portion, "tensor", scatter_dimension=1, tiled=True
    )
    grad_up_mine, grad_down_mine, grad_upbias_mine = (gradient_up_weight, grad_down, grad_up_bias)
    grad_summed, grad_gain_one, grad_shift_one = first_pull(grad_normed)
    grad_out_bias = jnp.sum(grad_summed, axis=(0, 1))
    gradient_rows_first = lax.all_gather(
        grad_summed.astype(jnp.bfloat16), "tensor", axis=1, tiled=True
    )
    grad_out_rows = jnp.einsum(
        "qwo,qwk->ok", context_merged, gradient_rows_first, preferred_element_type=jnp.float32
    )
    grad_context = jnp.einsum(
        "xpc,vc->xpv", gradient_rows_first, output_rows, preferred_element_type=jnp.float32
    )
    grad_context = grad_context.astype(jnp.bfloat16).reshape(sequences, length, heads, HD)
    gradient_query_rows, gradient_key_rows, gradient_value_rows = attention_backward(
        queries, key_heads, value_heads, segment_ids, logsums, grad_context, block, scale
    )
    flat_shape = (sequences, length, heads * HD)
    gradient_query_rows = gradient_query_rows.reshape(flat_shape)
    gradient_key_rows = gradient_key_rows.reshape(flat_shape)
    gradient_value_rows = gradient_value_rows.reshape(flat_shape)
    grad_query_cols = jnp.einsum(
        "hgb,hgu->bu", collected_rows, gradient_query_rows, preferred_element_type=jnp.float32
    )
    grad_key_cols = jnp.einsum(
        "hgb,hgu->bu", collected_rows, gradient_key_rows, preferred_element_type=jnp.float32
    )
    grad_value_cols = jnp.einsum(
        "hgb,hgu->bu", collected_rows, gradient_value_rows, preferred_element_type=jnp.float32
    )
    grad_query_bias = jnp.sum(gradient_query_rows, axis=(0, 1), dtype=jnp.float32).reshape(
        heads, HD
    )
    grad_value_bias = jnp.sum(gradient_value_rows, axis=(0, 1), dtype=jnp.float32).reshape(
        heads, HD
    )
    input_part = jnp.einsum(
        "vgr,hr->vgh", gradient_query_rows, query_columns, preferred_element_type=jnp.float32
    )
    input_part = input_part + jnp.einsum(
        "vgr,hr->vgh", gradient_key_rows, key_columns, preferred_element_type=jnp.float32
    )
    input_part = input_part + jnp.einsum(
        "vgr,hr->vgh", gradient_value_rows, value_columns, preferred_element_type=jnp.float32
    )
    grad_tokens = grad_summed + lax.psum_scatter(
        input_part.astype(jnp.bfloat16), "tensor", scatter_dimension=1, tiled=True
    ).astype(jnp.float32)
    weight_grads = (
        lax.psum_scatter(grad_query_cols, "dp", scatter_dimension=0, tiled=True),
        lax.psum_scatter(grad_key_cols, "dp", scatter_dimension=0, tiled=True),
        lax.psum_scatter(grad_value_cols, "dp", scatter_dimension=0, tiled=True),
        lax.psum_scatter(grad_out_rows, "dp", scatter_dimension=1, tiled=True),
        lax.psum_scatter(grad_query_bias, "dp", scatter_dimension=1, tiled=True),
        lax.psum_scatter(grad_value_bias, "dp", scatter_dimension=1, tiled=True),
        lax.psum_scatter(grad_up_mine, "dp", scatter_dimension=0, tiled=True),
        lax.psum_scatter(grad_down_mine, "dp", scatter_dimension=1, tiled=True),
        lax.psum_scatter(grad_upbias_mine, "dp", scatter_dimension=1, tiled=True),
    )
    vector_grads = (
        lax.psum_scatter(grad_out_bias, ("dp", "tensor"), scatter_dimension=0, tiled=True),
        lax.psum_scatter(grad_gain_one, ("dp", "tensor"), scatter_dimension=0, tiled=True),
        lax.psum_scatter(grad_shift_one, ("dp", "tensor"), scatter_dimension=0, tiled=True),
        lax.psum_scatter(grad_down_bias, ("dp", "tensor"), scatter_dimension=0, tiled=True),
        lax.psum_scatter(grad_gain_two, ("dp", "tensor"), scatter_dimension=0, tiled=True),
        lax.psum_scatter(grad_shift_two, ("dp", "tensor"), scatter_dimension=0, tiled=True),
    )
    return (
        layer_out,
        grad_tokens,
        weight_grads[0],
        weight_grads[1],
        weight_grads[2],
        weight_grads[3],
        weight_grads[4],
        weight_grads[5],
        weight_grads[6],
        weight_grads[7],
        weight_grads[8],
        vector_grads[0],
        vector_grads[1],
        vector_grads[2],
        vector_grads[3],
        vector_grads[4],
        vector_grads[5],
    )


def solution(mesh):
    in_specs = (
        P("dp", "tensor", None),
        P("dp", None),
        P("dp", "tensor"),
        P("dp", "tensor"),
        P("dp", "tensor"),
        P("tensor", "dp"),
        P("tensor", "dp"),
        P("tensor", "dp"),
        P("dp", "tensor"),
        P("tensor", "dp"),
        P("tensor", "dp"),
        P(("dp", "tensor")),
        P(("dp", "tensor")),
        P(("dp", "tensor")),
        P(("dp", "tensor")),
        P(("dp", "tensor")),
        P(("dp", "tensor")),
        P("dp", "tensor", None),
    )
    out_specs = (
        P("dp", "tensor", None),
        P("dp", "tensor", None),
        P("dp", "tensor"),
        P("dp", "tensor"),
        P("dp", "tensor"),
        P("tensor", "dp"),
        P("tensor", "dp"),
        P("tensor", "dp"),
        P("dp", "tensor"),
        P("tensor", "dp"),
        P("tensor", "dp"),
        P(("dp", "tensor")),
        P(("dp", "tensor")),
        P(("dp", "tensor")),
        P(("dp", "tensor")),
        P(("dp", "tensor")),
        P(("dp", "tensor")),
    )
    return jax.shard_map(
        per_device, mesh=mesh, in_specs=in_specs, out_specs=out_specs, check_vma=False
    )
```

profile of v0, /device:TPU:0, one launch (start us, length us, event | category | flops | bytes accessed | tf_op | source)
XLA Modules:
  0.0 1760.0 jit_solution(9406655017874332390)
XLA Ops:
  8.8 22.6 %all-gather.1 = bf16[8,8,3]{1,2,0:T(4,128)(2,1)S(1)} all-gather(bf16[1,8,3]{1,2,0:T(4,128)(2,1)} %bitcast.262), channel_id=1, replica_groups=mesh['dp'=8,'tensor'=4] {'dp'}, dimensions={0}, use_global_device_ids=true | all-gather | bytes 432 | tf_op jit(solution)/shard_map/all_gather | solution.py:150
  31.6 16.6 all-gather
  49.2 31.1 %all_gather.63 = bf16[192,768]{0,1:T(8,128)(2,1)S(1)} all-gather(bf16[192,96]{0,1:T(8,128)(2,1)S(1)} %copy.124), channel_id=1, replica_groups=mesh['dp'=8,'tensor'=4] {'dp'}, dimensions={1}, use_global_device_ids=true | all-gather | bytes 331776 | tf_op jit(solution)/shard_map/all_gather | solution.py:149
  80.4 31.2 %all_gather.60 = bf16[768,192]{1,0:T(8,128)(2,1)S(1)} all-gather(bf16[96,192]{1,0:T(8,128)(2,1)} %param.26), channel_id=1, replica_groups=mesh['dp'=8,'tensor'=4] {'dp'}, dimensions={0}, use_global_device_ids=true | all-gather | bytes 331776 | tf_op jit(solution)/shard_map/all_gather | solution.py:146
  111.5 31.4 %all_gather.62 = bf16[768,192]{1,0:T(8,128)(2,1)S(1)} all-gather(bf16[96,192]{1,0:T(8,128)(2,1)} %param.27), channel_id=1, replica_groups=mesh['dp'=8,'tensor'=4] {'dp'}, dimensions={0}, use_global_device_ids=true | all-gather | bytes 331776 | tf_op jit(solution)/shard_map/all_gather | solution.py:147
  142.9 31.2 %all_gather.58 = bf16[768,192]{1,0:T(8,128)(2,1)S(1)} all-gather(bf16[96,192]{1,0:T(8,128)(2,1)} %param.28), channel_id=1, replica_groups=mesh['dp'=8,'tensor'=4] {'dp'}, dimensions={0}, use_global_device_ids=true | all-gather | bytes 331776 | tf_op jit(solution)/shard_map/all_gather | solution.py:148
  187.4 225.8 %while.66 = (s32[]{:T(128)}, bf16[8,512,3,64]{1,3,2,0:T(8,128)(2,1)S(1)}, f32[8,3,512]{2,1,0:T(4,128)}, s32[8]{0:T(128)S(1)}, bf16[2,2048,3,64]{1,3,2,0:T(8,128)...) while((s32[]{:T(128)}, ...), condition=%wide.region_3.4_spmd, body=%wide.region_0.3_spmd.sunk | while | flops 844200448 | bytes 43995644 | solution.py:49
  193.3 8.4 fusion.133
  201.7 6.8 fusion.134
  208.5 7.0 fusion.135
  221.4 8.4 fusion.133
  229.9 6.8 fusion.134
  236.6 7.0 fusion.135
  249.6 8.4 fusion.133
  258.0 6.8 fusion.134
  264.8 7.0 fusion.135
  277.7 8.4 fusion.133
  286.2 6.8 fusion.134
  292.9 7.0 fusion.135
  305.9 8.4 fusion.133
  314.3 6.8 fusion.134
  321.1 7.0 fusion.135
  334.0 8.4 fusion.133
  342.5 6.8 fusion.134
  349.2 7.0 fusion.135
  362.2 8.4 fusion.133
  370.6 6.8 fusion.134
  377.4 7.0 fusion.135
  390.4 8.4 fusion.133
  398.8 6.8 fusion.134
  405.5 7.0 fusion.135
  417.2 6.8 fusion.59
  426.1 39.3 %all-reduce.17 = (bf16[768]{0:T(1024)(128)(2,1)S(1)}, bf16[768]{0:T(1024)(128)(2,1)S(1)}, bf16[768]{0:T(1024)(128)(2,1)S(1)}, bf16[768]{0:T(1024)(128)(2,1)}, bf...) all-reduce(bf16[768]{0:T(1024)(128)(2,1)S(1)} %dynamic-update-slice, ...), channel_id=1, replica_groups=mesh['dp'=8,'tensor'=4] {'dp','tensor'}, use_global_device_ids=true, to_apply=%add | all-reduce | flops 4608 | bytes 18432
  465.4 57.9 %reduce-scatter.22.cloned.1.call-done = f32[2,512,768]{2,1,0:T(8,128)} async-done(((f32[2,2048,768]{2,1,0:T(8,128)}), f32[2,512,768]{2,1,0:T(8,128)}) %reduce-scatter.22.cloned.1.call-update) | async-done | bytes 3145744 | tf_op jit(solution)/shard_map/reduce_scatter | solution.py:190
  529.6 27.0 %all_gather.69 = bf16[12,64]{0,1:T(8,128)(2,1)} all-gather(bf16[12,8]{0,1:T(8,128)(2,1)} %param.34), channel_id=1, replica_groups=mesh['dp'=8,'tensor'=4] {'dp'}, dimensions={1}, use_global_device_ids=true | all-gather | bytes 1728 | tf_op jit(solution)/shard_map/all_gather | solution.py:154
  559.3 16.0 all-gather.11.cloned.1.call-done
  575.3 13.5 fusion.55
  593.2 31.8 %multiply_convert_fusion.1 = (bf16[2,2048,768]{2,1,0:T(8,128)(2,1)}, f32[2,2048,768]{2,1,0:T(8,128)}) fusion(f32[2,2048,768]{2,1,0:T(8,128)S(1)} %get-tuple-element.838, f32[768]{0:T(1024)S(1)} %copy-done.31, u8[2048,768]{1,0:T(8,128)(4,1)} %get-tuple-element.728, u8[2048,768]{1,0:T(8,128)(4,1)} %get-tuple-element.727), kind=kLoop, calls=%fused_computation.72 | loop fusion | flops 223346688 | bytes 34606080 | tf_op jit(solution)/shard_map/convert_element_type | solution.py:201
  625.1 10.2 fusion.65
  639.2 95.7 %reduce-scatter.24.cloned.1.call-done = f32[2,512,768]{2,1,0:T(8,128)} async-done(((f32[2,2048,768]{2,1,0:T(8,128)}), f32[2,512,768]{2,1,0:T(8,128)}) %reduce-scatter.24.cloned.1.call-update) | async-done | bytes 3145744 | tf_op jit(solution)/shard_map/reduce_scatter | solution.py:205
  747.4 46.5 %all-gather.17.cloned.1.call-done = bf16[2,2048,768]{2,1,0:T(8,128)(2,1)} async-done(((bf16[2,512,768]{2,1,0:T(8,128)(2,1)}), bf16[2,2048,768]{2,1,0:T(8,128)(2,1)}) %all-gather.17.cloned.1.call-update) | async-done | bytes 6291472 | tf_op jit(solution)/shard_map/all_gather | solution.py:212
  793.9 17.3 convert_reduce_fusion
  811.2 10.6 fusion.67
  821.9 99.8 %reduce-scatter.26.cloned.1.call-done = f32[2,512,768]{2,1,0:T(8,128)} async-done(((f32[2,2048,768]{2,1,0:T(8,128)}), f32[2,512,768]{2,1,0:T(8,128)}) %reduce-scatter.26.cloned.1.call-update) | async-done | bytes 3145744 | tf_op jit(solution)/shard_map/reduce_scatter | solution.py:227
  930.9 46.4 %all-gather.19.cloned.1.call-done = bf16[2,2048,768]{2,1,0:T(8,128)(2,1)} async-done(((bf16[2,512,768]{2,1,0:T(8,128)(2,1)}), bf16[2,2048,768]{2,1,0:T(8,128)(2,1)}) %all-gather.19.cloned.1.call-update) | async-done | bytes 6291472 | tf_op jit(solution)/shard_map/all_gather | solution.py:233
  977.4 6.4 fusion.61
  990.5 326.1 %while.68 = (s32[]{:T(128)}, bf16[2,2048,3,64]{3,2,1,0:T(4,128)(2,1)}, bf16[2,2048,3,64]{1,3,2,0:T(8,128)(2,1)}, bf16[2,2048,3,64]{1,3,2,0:T(8,128)(2,1)}, s32[2...) while((s32[]{:T(128)}, ...), condition=%wide.region_19.20_spmd, body=%wide.region_15.19_spmd.sunk | while | flops 2064448000 | bytes 176434160 | solution.py:112
  997.9 144.7 %while.69 = (s32[]{:T(128)}, f32[2048,3,64]{0,2,1:T(8,128)}, f32[2048,3,64]{0,2,1:T(8,128)}, bf16[4,512,3,64]{1,3,2,0:T(8,128)(2,1)}, s32[4]{0:T(128)S(1)}, /*in...) while((s32[]{:T(128)}, f32[2048,3,64]{0,2,1:T(8,128)}, ...), condition=%wide.region_18.18_spmd.clone, body=%wide.region_16.17_spmd.clone.sunk | while | flops 2063661568 | bytes 143911376 | solution.py:103
  1041.2 6.4 fusion.147
  1077.7 6.4 fusion.147
  1160.8 144.7 %while.69 = (s32[]{:T(128)}, f32[2048,3,64]{0,2,1:T(8,128)}, f32[2048,3,64]{0,2,1:T(8,128)}, bf16[4,512,3,64]{1,3,2,0:T(8,128)(2,1)}, s32[4]{0:T(128)S(1)}, /*in...) while((s32[]{:T(128)}, f32[2048,3,64]{0,2,1:T(8,128)}, ...), condition=%wide.region_18.18_spmd.clone, body=%wide.region_16.17_spmd.clone.sunk | while | flops 2063661568 | bytes 143911376 | solution.py:103
  1204.1 6.4 fusion.147
  1240.6 6.4 fusion.147
  1322.2 6.4 fusion.73
  1328.6 6.4 fusion.76
  1335.0 12.1 add_convert_fusion
  1347.1 10.1 convolution_bitcast_fusion.1
  1357.3 10.9 convolution_bitcast_fusion
  1383.8 41.3 %all-reduce.15 = (f32[768]{0:T(1024)S(1)}, f32[768]{0:T(1024)S(1)}, f32[768]{0:T(1024)S(1)}, f32[768]{0:T(1024)S(1)}, f32[768]{0:T(1024)S(1)}, /*index=5*/f32[768]{0:T(1024)S(1)}) all-reduce(f32[768]{0:T(1024)S(1)} %copy-done.36, f32[768]{0:T(1024)S(1)} %copy-done.29, ...), channel_id=15, replica_groups=mesh['dp'=8,'tensor'=4] {'dp','tensor'}, use_global_device_ids=true, to_apply=%region_34.35.clone | all-reduce | flops 4608 | bytes 36864
  1443.7 37.5 %all-reduce.16 = (f32[3,64]{1,0:T(4,128)S(1)}, f32[3,64]{1,0:T(4,128)S(1)}, f32[12,64]{1,0:T(8,128)S(1)}) all-reduce(f32[3,64]{1,0:T(4,128)S(1)} %convert_reduce_fusion.1, f32[3,64]{1,0:T(4,128)S(1)} %convert_reduce_fusion.2, f32[12,64]{1,0:T(8,128)S(1)} %reshape.284), channel_id=10, replica_groups=mesh['dp'=8,'tensor'=4] {'dp'}, use_global_device_ids=true, to_apply=%region_26.27.clone | all-reduce | flops 1152 | bytes 9216
  1487.7 66.1 %reduce-scatter.32.cloned.1.call-done = f32[768,96]{0,1:T(8,128)} async-done(((f32[768,768]{0,1:T(8,128)}), f32[768,96]{0,1:T(8,128)}) %reduce-scatter.32.cloned.1.call-update) | async-done | bytes 294928 | tf_op jit(solution)/shard_map/reduce_scatter | solution.py:285
  1553.7 66.4 %reduce-scatter.34.cloned.1.call-done = f32[96,192]{1,0:T(8,128)} async-done(((f32[768,192]{1,0:T(8,128)}), f32[96,192]{1,0:T(8,128)}) %reduce-scatter.34.cloned.1.call-update) | async-done | bytes 73744
  1620.1 66.1 %reduce-scatter.36.cloned.1.call-done = f32[96,192]{1,0:T(8,128)} async-done(((f32[768,192]{1,0:T(8,128)}), f32[96,192]{1,0:T(8,128)}) %reduce-scatter.36.cloned.1.call-update) | async-done | bytes 73744
  1686.2 66.2 %reduce-scatter.38.cloned.1.call-done = f32[96,192]{1,0:T(8,128)} async-done(((f32[768,192]{1,0:T(8,128)}), f32[96,192]{1,0:T(8,128)}) %reduce-scatter.38.cloned.1.call-update) | async-done | bytes 73744
  (411 shorter events, 414.5 us)
Async XLA Ops:
  8.0 166.1 %all-gather.9.cloned.1.call-start = ((), (), s32[]{:S(2)}) async-start(), calls=%async_computation.10 | async-start | bytes 7864320 | tf_op jit(solution)/shard_map/all_gather | solution.py:167
  8.8 514.6 %reduce-scatter.22.cloned.1.call-start = ((), (), s32[]{:S(2)}) async-start(), calls=%async_computation.11 | async-start | bytes 15728640 | tf_op jit(solution)/shard_map/reduce_scatter | solution.py:190
  111.5 72.4 %copy-start.22 = (bf16[768,192]{1,0:T(8,128)(2,1)}, bf16[768,192]{1,0:T(8,128)(2,1)S(1)}, u32[]{:S(2)}) copy-start(bf16[768,192]{1,0:T(8,128)(2,1)S(1)} %all_gather.60) | copy-start | bytes 884740
  142.9 41.0 %copy-start.16 = (bf16[768,192]{1,0:T(8,128)(2,1)}, bf16[768,192]{1,0:T(8,128)(2,1)S(1)}, u32[]{:S(2)}) copy-start(bf16[768,192]{1,0:T(8,128)(2,1)S(1)} %all_gather.62) | copy-start | bytes 884740
  174.1 9.8 copy-start.18
  174.1 6.4 copy-start.15
  417.2 6.8 copy-start.13
  424.1 135.2 %all-gather.13.cloned.1.call-start = ((), (), s32[]{:S(2)}) async-start(), calls=%async_computation.13 | async-start | bytes 1327104 | tf_op jit(solution)/shard_map/all_gather | solution.py:152
  424.7 150.6 %all-gather.11.cloned.1.call-start = ((), (), s32[]{:S(2)}) async-start(), calls=%async_computation.12 | async-start | bytes 7864320 | tf_op jit(solution)/shard_map/all_gather | solution.py:194
  529.0 96.1 %all-gather.15.cloned.1.call-start = ((), (), s32[]{:S(2)}) async-start(), calls=%async_computation.14 | async-start | bytes 1327104 | tf_op jit(solution)/shard_map/all_gather | solution.py:153
  529.5 205.4 %reduce-scatter.24.cloned.1.call-start = ((), (), s32[]{:S(2)}) async-start(), calls=%async_computation.15 | async-start | bytes 15728640 | tf_op jit(solution)/shard_map/reduce_scatter | solution.py:205
  575.3 17.9 %copy-start.31 = (f32[768]{0:T(1024)S(1)}, f32[768]{0:T(1024)}, u32[]{:S(2)}) copy-start(f32[768]{0:T(1024)} %reshape.287) | copy-start | bytes 9220
  588.7 4.5 copy-start.8
  635.3 158.5 %all-gather.17.cloned.1.call-start = ((), (), s32[]{:S(2)}) async-start(), calls=%async_computation.16 | async-start | bytes 7864320 | tf_op jit(solution)/shard_map/all_gather | solution.py:212
  747.3 174.3 %reduce-scatter.26.cloned.1.call-start = ((), (), s32[]{:S(2)}) async-start(), calls=%async_computation.17 | async-start | bytes 15728640 | tf_op jit(solution)/shard_map/reduce_scatter | solution.py:227
  793.8 17.3 copy-start.38
  821.8 155.5 %all-gather.19.cloned.1.call-start = ((), (), s32[]{:S(2)}) async-start(), calls=%async_computation.18 | async-start | bytes 7864320 | tf_op jit(solution)/shard_map/all_gather | solution.py:233
  921.6 4.3 copy-start.28
  927.1 50.2 %copy-start.14 = (bf16[2,2048,192]{1,0,2:T(2,128)(2,1)S(1)}, bf16[2,2048,192]{1,0,2:T(2,128)(2,1)}, u32[]{:S(2)}) copy-start(bf16[2,2048,192]{1,0,2:T(2,128)(2,1)} %copy-done.13) | copy-start | bytes 4718596
  927.1 56.6 %copy-start.24 = (f32[2,512]{1,0:T(2,128)}, f32[2,512]{1,0:T(2,128)S(1)}, u32[]{:S(2)}) copy-start(f32[2,512]{1,0:T(2,128)S(1)} %negate_multiply_fusion.1) | copy-start | bytes 12292
  930.9 551.7 %reduce-scatter.40.cloned.1.call-start = ((), (), s32[]{:S(2)}) async-start(), calls=%async_computation.25 | async-start | bytes 884736
  983.8 500.4 %reduce-scatter.28.cloned.1.call-start = ((), (), s32[]{:S(2)}) async-start(), calls=%async_computation.19 | async-start | bytes 7864320 | tf_op jit(solution)/shard_map/reduce_scatter | solution.py:274
  990.5 331.7 %copy-start.17 = (bf16[768,192]{1,0:T(8,128)(2,1)S(1)}, bf16[768,192]{1,0:T(8,128)(2,1)}, u32[]{:S(2)}) copy-start(bf16[768,192]{1,0:T(8,128)(2,1)} %copy-done.16) | copy-start | bytes 884740
  997.9 7.9 copy-start.2
  1023.9 5.8 copy-start
  1033.3 7.9 copy-start.2
  1059.9 5.8 copy-start
  1069.8 7.9 copy-start.2
  1096.4 5.8 copy-start
  1102.2 4.1 copy-start.3
  1106.3 7.8 copy-start.2
  1132.8 5.8 copy-start
  1142.7 7.2 copy-start.4
  1142.7 7.2 copy-start.10
  1160.8 7.9 copy-start.2
  1186.8 5.8 copy-start
  1196.2 7.9 copy-start.2
  1222.7 5.8 copy-start
  1232.7 7.9 copy-start.2
  1259.2 5.8 copy-start
  1265.0 4.1 copy-start.3
  1269.2 7.8 copy-start.2
  1295.6 5.8 copy-start
  1305.5 7.2 copy-start.4
  1305.5 7.2 copy-start.10
  1316.6 5.6 copy-start.20
  1322.2 6.4 copy-start.23
  1328.6 6.4 copy-start.12
  1328.6 6.4 copy-start.19
  1347.1 140.6 %reduce-scatter.30.cloned.1.call-start = ((), (), s32[]{:S(2)}) async-start(), calls=%async_computation.20 | async-start | bytes 2654208 | tf_op jit(solution)/shard_map/reduce_scatter | solution.py:284
  1357.2 196.5 %reduce-scatter.32.cloned.1.call-start = ((), (), s32[]{:S(2)}) async-start(), calls=%async_computation.21 | async-start | bytes 2654208 | tf_op jit(solution)/shard_map/reduce_scatter | solution.py:285
  1368.2 252.0 %reduce-scatter.34.cloned.1.call-start = ((), (), s32[]{:S(2)}) async-start(), calls=%async_computation.22 | async-start | bytes 884736
  1376.1 6.3 copy-start.45
  1376.2 7.6 copy-start.37
  1376.2 7.6 copy-start.29
  1376.2 7.6 copy-start.30
  1376.2 7.6 copy-start.33
  1376.2 7.6 copy-start.34
  1376.2 7.6 copy-start.35
  1376.2 7.6 copy-start.36
  1376.2 310.0 %reduce-scatter.36.cloned.1.call-start = ((), (), s32[]{:S(2)}) async-start(), calls=%async_computation.23 | async-start | bytes 884736
  1382.4 370.1 %reduce-scatter.38.cloned.1.call-start = ((), (), s32[]{:S(2)}) async-start(), calls=%async_computation.24 | async-start | bytes 884736
  1433.8 50.4 %copy-start.6 = (f32[2,512,768]{2,1,0:T(8,128)S(1)}, f32[2,512,768]{2,1,0:T(8,128)}, u32[]{:S(2)}) copy-start(f32[2,512,768]{2,1,0:T(8,128)} %copy-done.5) | copy-start | bytes 9437188
  1433.8 50.4 %copy-start.25 = (f32[2,512]{1,0:T(2,128)S(1)}, f32[2,512]{1,0:T(2,128)}, u32[]{:S(2)}) copy-start(f32[2,512]{1,0:T(2,128)} %copy-done.24) | copy-start | bytes 12292
  (29 other events, 74.5 us)
Sparse Core Ops, SparseCore 0:
  10.4 49.0 all-gather.8
  424.2 99.0 reduce-scatter.21
  747.4 46.3 all-gather.16
  931.0 46.3 all-gather.18
Sparse Core Ops, SparseCore 1:
  426.7 40.1 all-gather.12
  529.0 46.2 all-gather.10
  577.3 41.4 all-gather.14
  635.4 99.5 reduce-scatter.23
  821.9 99.7 reduce-scatter.25
  983.9 63.3 reduce-scatter.39
  1347.2 59.4 reduce-scatter.27
  1410.6 69.9 reduce-scatter.29
  1484.5 69.1 reduce-scatter.31
  1557.6 62.5 reduce-scatter.33
  1623.9 62.3 reduce-scatter.35
  1690.1 62.3 reduce-scatter.37
where the time goes:
time: 1770 us; the launch traced here: 1760 us
  waiting for transfers between devices  629 us (36%)
  matrix products  471 us (27%)
  blocking collectives  309 us (17%)
  other arithmetic  193 us (11%)
  local copies, waits for them, and re-layouts  92.6 us (5%)
  loops' own time  47.2 us (3%)
    unnamed x20, waiting for transfers between devices  201 us
    unnamed x3, blocking collectives  118 us
    reduce_scatter x1, waiting for transfers between devices, per_device(): lax.psum_scatter(backward_portion, 'tensor', scatter_dimension=1, tiled=T...  99.8 us
    reduce_scatter x1, waiting for transfers between devices, per_device(): lax.psum_scatter(branch_part, 'tensor', scatter_dimension=1, tiled=True)  95.7 us
    dot_general x16, matrix products, block_scores(): jnp.einsum('qhd,khd->hqk', query_rows, key_heads, preferred_element_type=...  92.9 us
    reduce_scatter x1, waiting for transfers between devices, per_device(): lax.psum_scatter(grad_down_mine, 'dp', scatter_dimension=1, tiled=True)  66.1 us
    reduce_scatter x1, waiting for transfers between devices, per_device(): lax.psum_scatter(partial_out, 'tensor', scatter_dimension=1, tiled=True)  57.9 us
    dot_general x8, matrix products, one_block(): jnp.einsum('hqk,khd->qhd', weights, value_heads[which], preferred_element...  55.7 us
  transfers between devices with their start and end apart: 16, of which 10 were waited for; matrix products, arithmetic and copies ran while one was open for 26% of the time, Pallas kernels for 0%

commit v1 on v0

--- a/solution.py
+++ b/solution.py
@@ -209,7 +209,24 @@
     grad_sum_two, grad_gain_two, grad_shift_two = second_pull(cotangent)
     grad_down_bias = jnp.sum(grad_sum_two, axis=(0, 1))
     grad_branch = grad_sum_two.astype(jnp.bfloat16)
-    gradient_branch_total = lax.all_gather(grad_branch, "tensor", axis=1, tiled=True)
+    ways, here, step = (lax.axis_size("tensor"), lax.axis_index("tensor"), grad_branch.shape[1])
+    shape = [n * ways if d == 1 else n for d, n in enumerate(grad_branch.shape)]
+    gradient_branch_total = lax.dynamic_update_slice_in_dim(
+        jnp.zeros(shape, grad_branch.dtype), grad_branch, here * step, axis=1
+    )
+    going_up = going_down = grad_branch
+    for far in range(1, ways // 2 + 1):
+        going_up = lax.ppermute(going_up, "tensor", [(d, (d + 1) % ways) for d in range(ways)])
+        gradient_branch_total = lax.dynamic_update_slice_in_dim(
+            gradient_branch_total, going_up, (here - far) % ways * step, axis=1
+        )
+        if 2 * far < ways:
+            going_down = lax.ppermute(
+                going_down, "tensor", [(d, (d - 1) % ways) for d in range(ways)]
+            )
+            gradient_branch_total = lax.dynamic_update_slice_in_dim(
+                gradient_branch_total, going_down, (here + far) % ways * step, axis=1
+            )
     grad_down = jnp.einsum(
         "ypw,ypv->wv", activated_reduced, gradient_branch_total, preferred_element_type=jnp.float32
     )

time: 1770 us -> 1790 us (1.011)
  local copies, waits for them, and re-layouts: 92.6 us -> 116 us
    all_gather x1 -> x0, waiting for transfers between devices: 46.5 us -> none  [per_device(): lax.all_gather(grad_branch, 'tensor', axis=1, tiled=True)]
    ppermute x0 -> x3, waiting for transfers between devices: none -> 36.8 us  [the longest x2 36.8 us: per_device(): lax.ppermute(going_up, 'tensor', [(d, (d + 1) % ways) for d in range(ways)])]
    unnamed x20 -> x19, waiting for transfers between devices: 201 us -> 201 us
  transfers between devices with their start and end apart: 16 -> 18, of which waited for: 10 -> 11; matrix products, arithmetic and copies ran while one was open for 26% -> 27% of each run, Pallas kernels for 0% -> 0%
where the time goes in v1:
time: 1790 us; the launch traced here: 1780 us
  waiting for transfers between devices  619 us (35%)
  matrix products  472 us (26%)
  blocking collectives  309 us (17%)
  other arithmetic  194 us (11%)
  local copies, waits for them, and re-layouts  116 us (6%)
  loops' own time  47.2 us (3%)
    unnamed x19, waiting for transfers between devices  201 us
    unnamed x3, blocking collectives  118 us
    reduce_scatter x1, waiting for transfers between devices, per_device(): lax.psum_scatter(backward_portion, 'tensor', scatter_dimension=1, tiled=T...  99.7 us
    reduce_scatter x1, waiting for transfers between devices, per_device(): lax.psum_scatter(branch_part, 'tensor', scatter_dimension=1, tiled=True)  95.9 us
    dot_general x16, matrix products, block_scores(): jnp.einsum('qhd,khd->hqk', query_rows, key_heads, preferred_element_type=...  92.8 us
    reduce_scatter x1, waiting for transfers between devices, per_device(): lax.psum_scatter(grad_down_mine, 'dp', scatter_dimension=1, tiled=True)  65.3 us
    reduce_scatter x1, waiting for transfers between devices, per_device(): lax.psum_scatter(partial_out, 'tensor', scatter_dimension=1, tiled=True)  57.9 us
    dot_general x8, matrix products, one_block(): jnp.einsum('hqk,khd->qhd', weights, value_heads[which], preferred_element...  55.7 us
  transfers between devices with their start and end apart: 18, of which 11 were waited for; matrix products, arithmetic and copies ran while one was open for 27% of the time, Pallas kernels for 0%

profile of v1, /device:TPU:0, one launch (start us, length us, event | category | flops | bytes accessed | tf_op | source)
XLA Modules:
  0.0 1775.5 jit_solution(11489797882300970648)
XLA Ops:
  8.8 22.6 %all-gather.1 = bf16[8,8,3]{1,2,0:T(4,128)(2,1)S(1)} all-gather(bf16[1,8,3]{1,2,0:T(4,128)(2,1)} %bitcast.262), channel_id=1, replica_groups=mesh['dp'=8,'tensor'=4] {'dp'}, dimensions={0}, use_global_device_ids=true | all-gather | bytes 432 | tf_op jit(solution)/shard_map/all_gather | solution.py:150
  31.6 16.6 all-gather
  49.2 31.1 %all_gather.60 = bf16[192,768]{0,1:T(8,128)(2,1)S(1)} all-gather(bf16[192,96]{0,1:T(8,128)(2,1)S(1)} %copy.140), channel_id=1, replica_groups=mesh['dp'=8,'tensor'=4] {'dp'}, dimensions={1}, use_global_device_ids=true | all-gather | bytes 331776 | tf_op jit(solution)/shard_map/all_gather | solution.py:149
  80.4 31.2 %all_gather.57 = bf16[768,192]{1,0:T(8,128)(2,1)S(1)} all-gather(bf16[96,192]{1,0:T(8,128)(2,1)} %param.26), channel_id=1, replica_groups=mesh['dp'=8,'tensor'=4] {'dp'}, dimensions={0}, use_global_device_ids=true | all-gather | bytes 331776 | tf_op jit(solution)/shard_map/all_gather | solution.py:146
  111.5 31.4 %all_gather.59 = bf16[768,192]{1,0:T(8,128)(2,1)S(1)} all-gather(bf16[96,192]{1,0:T(8,128)(2,1)} %param.27), channel_id=1, replica_groups=mesh['dp'=8,'tensor'=4] {'dp'}, dimensions={0}, use_global_device_ids=true | all-gather | bytes 331776 | tf_op jit(solution)/shard_map/all_gather | solution.py:147
  142.9 31.2 %all_gather.55 = bf16[768,192]{1,0:T(8,128)(2,1)S(1)} all-gather(bf16[96,192]{1,0:T(8,128)(2,1)} %param.28), channel_id=1, replica_groups=mesh['dp'=8,'tensor'=4] {'dp'}, dimensions={0}, use_global_device_ids=true | all-gather | bytes 331776 | tf_op jit(solution)/shard_map/all_gather | solution.py:148
  174.1 6.3 convolution_convert_fusion.1
  187.3 225.7 %while.66 = (s32[]{:T(128)}, bf16[8,512,3,64]{1,3,2,0:T(8,128)(2,1)S(1)}, f32[8,3,512]{2,1,0:T(4,128)}, s32[8]{0:T(128)S(1)}, bf16[2,2048,3,64]{1,3,2,0:T(8,128)...) while((s32[]{:T(128)}, ...), condition=%wide.region_3.4_spmd, body=%wide.region_0.3_spmd.sunk | while | flops 844200448 | bytes 43995644 | solution.py:49
  193.2 8.4 fusion.133
  201.6 6.8 fusion.134
  208.4 7.0 fusion.135
  221.4 8.4 fusion.133
  229.8 6.8 fusion.134
  236.6 7.0 fusion.135
  249.5 8.4 fusion.133
  257.9 6.8 fusion.134
  264.7 7.0 fusion.135
  277.7 8.4 fusion.133
  286.1 6.8 fusion.134
  292.8 7.0 fusion.135
  305.8 8.4 fusion.133
  314.2 6.8 fusion.134
  321.0 7.0 fusion.135
  334.0 8.4 fusion.133
  342.4 6.8 fusion.134
  349.1 7.0 fusion.135
  362.1 8.4 fusion.133
  370.5 6.8 fusion.134
  377.3 7.0 fusion.135
  390.3 8.4 fusion.133
  398.7 6.8 fusion.134
  405.4 7.0 fusion.135
  417.1 6.8 fusion.59
  426.1 39.3 %all-reduce.17 = (bf16[768]{0:T(1024)(128)(2,1)S(1)}, bf16[768]{0:T(1024)(128)(2,1)S(1)}, bf16[768]{0:T(1024)(128)(2,1)S(1)}, bf16[768]{0:T(1024)(128)(2,1)}, bf...) all-reduce(bf16[768]{0:T(1024)(128)(2,1)S(1)} %dynamic-update-slice, ...), channel_id=1, replica_groups=mesh['dp'=8,'tensor'=4] {'dp','tensor'}, use_global_device_ids=true, to_apply=%add | all-reduce | flops 4608 | bytes 18432
  465.3 57.9 %reduce-scatter.22.cloned.1.call-done = f32[2,512,768]{2,1,0:T(8,128)} async-done(((f32[2,2048,768]{2,1,0:T(8,128)}), f32[2,512,768]{2,1,0:T(8,128)}) %reduce-scatter.22.cloned.1.call-update) | async-done | bytes 3145744 | tf_op jit(solution)/shard_map/reduce_scatter | solution.py:190
  529.5 27.0 %all_gather.66 = bf16[12,64]{0,1:T(8,128)(2,1)} all-gather(bf16[12,8]{0,1:T(8,128)(2,1)} %param.34), channel_id=1, replica_groups=mesh['dp'=8,'tensor'=4] {'dp'}, dimensions={1}, use_global_device_ids=true | all-gather | bytes 1728 | tf_op jit(solution)/shard_map/all_gather | solution.py:154
  559.2 16.0 all-gather.10.cloned.1.call-done
  575.2 13.5 fusion.55
  593.1 31.8 %multiply_convert_fusion.1 = (bf16[2,2048,768]{2,1,0:T(8,128)(2,1)}, f32[2,2048,768]{2,1,0:T(8,128)}) fusion(f32[2,2048,768]{2,1,0:T(8,128)S(1)} %get-tuple-element.838, f32[768]{0:T(1024)S(1)} %copy-done.32, u8[2048,768]{1,0:T(8,128)(4,1)} %get-tuple-element.728, u8[2048,768]{1,0:T(8,128)(4,1)} %get-tuple-element.727), kind=kLoop, calls=%fused_computation.72 | loop fusion | flops 223346688 | bytes 34606080 | tf_op jit(solution)/shard_map/convert_element_type | solution.py:201
  625.0 10.2 fusion.65
  639.1 95.9 %reduce-scatter.24.cloned.1.call-done = f32[2,512,768]{2,1,0:T(8,128)} async-done(((f32[2,2048,768]{2,1,0:T(8,128)}), f32[2,512,768]{2,1,0:T(8,128)}) %reduce-scatter.24.cloned.1.call-update) | async-done | bytes 3145744 | tf_op jit(solution)/shard_map/reduce_scatter | solution.py:205
  749.2 34.6 %collective-permute-done = bf16[2,512,768]{2,1,0:T(8,128)(2,1)} collective-permute-done((bf16[2,512,768]{2,1,0:T(8,128)(2,1)}, bf16[2,512,768]{2,1,0:T(8,128)(2,1)}, u32[]{:S(2)}, u32[]{:S(2)}) %collective-permute-start) | collective-permute-done | bytes 1572896 | tf_op jit(solution)/shard_map/ppermute | solution.py:219
  809.3 18.0 %convert_reduce_fusion = (f32[768]{0:T(1024)}, bf16[2,2048,768]{2,1,0:T(8,128)(2,1)}) fusion(f32[2,2048,768]{2,1,0:T(8,128)} %get-tuple-element.824, bf16[2,2048,768]{1,2,0:T(8,128)(2,1)} %constant_dynamic-update-slice_fusion, bf16[768,768]{0,1:T(8,128)(2,1)} %all-gather.14.cloned.1.call-done, f32[2,2048,768]{2,1,0:T(8,128)} %copy-done.8, f32[768]{0:T(1024)} %reshape.287), kind=kOutput, calls=%fused_computation.69 | convolution fusion | flops 4885314560 | bytes 38934528 | tf_op jit(solution)/shard_map/mti,oi->mto/dot_general | solution.py:233
  827.3 10.6 fusion.67
  838.0 99.7 %reduce-scatter.26.cloned.1.call-done = f32[2,512,768]{2,1,0:T(8,128)} async-done(((f32[2,2048,768]{2,1,0:T(8,128)}), f32[2,512,768]{2,1,0:T(8,128)}) %reduce-scatter.26.cloned.1.call-update) | async-done | bytes 3145744 | tf_op jit(solution)/shard_map/reduce_scatter | solution.py:244
  947.1 46.3 %all-gather.16.cloned.1.call-done = bf16[2,2048,768]{2,1,0:T(8,128)(2,1)} async-done(((bf16[2,512,768]{2,1,0:T(8,128)(2,1)}), bf16[2,2048,768]{2,1,0:T(8,128)(2,1)}) %all-gather.16.cloned.1.call-update) | async-done | bytes 6291472 | tf_op jit(solution)/shard_map/all_gather | solution.py:250
  993.3 6.4 fusion.61
  1006.5 325.8 %while.68 = (s32[]{:T(128)}, bf16[2,2048,3,64]{3,2,1,0:T(4,128)(2,1)}, bf16[2,2048,3,64]{1,3,2,0:T(8,128)(2,1)}, bf16[2,2048,3,64]{1,3,2,0:T(8,128)(2,1)}, s32[2...) while((s32[]{:T(128)}, ...), condition=%wide.region_19.20_spmd, body=%wide.region_15.19_spmd.sunk | while | flops 2064448000 | bytes 176434160 | solution.py:112
  1013.9 144.6 %while.69 = (s32[]{:T(128)}, f32[2048,3,64]{0,2,1:T(8,128)}, f32[2048,3,64]{0,2,1:T(8,128)}, bf16[4,512,3,64]{1,3,2,0:T(8,128)(2,1)}, s32[4]{0:T(128)S(1)}, /*in...) while((s32[]{:T(128)}, f32[2048,3,64]{0,2,1:T(8,128)}, ...), condition=%wide.region_18.18_spmd.clone, body=%wide.region_16.17_spmd.clone.sunk | while | flops 2063661568 | bytes 143911376 | solution.py:103
  1093.6 6.3 fusion.147
  1176.6 144.6 %while.69 = (s32[]{:T(128)}, f32[2048,3,64]{0,2,1:T(8,128)}, f32[2048,3,64]{0,2,1:T(8,128)}, bf16[4,512,3,64]{1,3,2,0:T(8,128)(2,1)}, s32[4]{0:T(128)S(1)}, /*in...) while((s32[]{:T(128)}, f32[2048,3,64]{0,2,1:T(8,128)}, ...), condition=%wide.region_18.18_spmd.clone, body=%wide.region_16.17_spmd.clone.sunk | while | flops 2063661568 | bytes 143911376 | solution.py:103
  1219.8 6.3 fusion.147
  1256.3 6.3 fusion.147
  1337.8 6.4 fusion.73
  1344.3 6.4 fusion.76
  1350.6 12.1 add_convert_fusion
  1362.8 10.1 convolution_bitcast_fusion.1
  1372.9 12.4 convolution_bitcast_fusion
  1400.1 41.4 %all-reduce.15 = (f32[768]{0:T(1024)S(1)}, f32[768]{0:T(1024)S(1)}, f32[768]{0:T(1024)S(1)}, f32[768]{0:T(1024)S(1)}, f32[768]{0:T(1024)S(1)}, /*index=5*/f32[768]{0:T(1024)S(1)}) all-reduce(f32[768]{0:T(1024)S(1)} %copy-done.37, f32[768]{0:T(1024)S(1)} %copy-done.30, ...), channel_id=15, replica_groups=mesh['dp'=8,'tensor'=4] {'dp','tensor'}, use_global_device_ids=true, to_apply=%region_34.35.clone | all-reduce | flops 4608 | bytes 36864
  1460.0 37.4 %all-reduce.16 = (f32[3,64]{1,0:T(4,128)S(1)}, f32[3,64]{1,0:T(4,128)S(1)}, f32[12,64]{1,0:T(8,128)S(1)}) all-reduce(f32[3,64]{1,0:T(4,128)S(1)} %convert_reduce_fusion.1, f32[3,64]{1,0:T(4,128)S(1)} %convert_reduce_fusion.2, f32[12,64]{1,0:T(8,128)S(1)} %reshape.284), channel_id=10, replica_groups=mesh['dp'=8,'tensor'=4] {'dp'}, use_global_device_ids=true, to_apply=%region_26.27.clone | all-reduce | flops 1152 | bytes 9216
  1503.9 65.3 %reduce-scatter.32.cloned.1.call-done = f32[768,96]{0,1:T(8,128)} async-done(((f32[768,768]{0,1:T(8,128)}), f32[768,96]{0,1:T(8,128)}) %reduce-scatter.32.cloned.1.call-update) | async-done | bytes 294928 | tf_op jit(solution)/shard_map/reduce_scatter | solution.py:302
  1569.2 66.4 %reduce-scatter.34.cloned.1.call-done = f32[96,192]{1,0:T(8,128)} async-done(((f32[768,192]{1,0:T(8,128)}), f32[96,192]{1,0:T(8,128)}) %reduce-scatter.34.cloned.1.call-update) | async-done | bytes 73744
  1635.6 66.1 %reduce-scatter.36.cloned.1.call-done = f32[96,192]{1,0:T(8,128)} async-done(((f32[768,192]{1,0:T(8,128)}), f32[96,192]{1,0:T(8,128)}) %reduce-scatter.36.cloned.1.call-update) | async-done | bytes 73744
  1701.7 66.2 %reduce-scatter.38.cloned.1.call-done = f32[96,192]{1,0:T(8,128)} async-done(((f32[768,192]{1,0:T(8,128)}), f32[96,192]{1,0:T(8,128)}) %reduce-scatter.38.cloned.1.call-update) | async-done | bytes 73744
  (425 shorter events, 440.8 us)
Async XLA Ops:
  8.0 166.1 %all-gather.8.cloned.1.call-start = ((), (), s32[]{:S(2)}) async-start(), calls=%async_computation.10 | async-start | bytes 7864320 | tf_op jit(solution)/shard_map/all_gather | solution.py:167
  8.8 514.5 %reduce-scatter.22.cloned.1.call-start = ((), (), s32[]{:S(2)}) async-start(), calls=%async_computation.11 | async-start | bytes 15728640 | tf_op jit(solution)/shard_map/reduce_scatter | solution.py:190
  111.5 72.3 %copy-start.23 = (bf16[768,192]{1,0:T(8,128)(2,1)}, bf16[768,192]{1,0:T(8,128)(2,1)S(1)}, u32[]{:S(2)}) copy-start(bf16[768,192]{1,0:T(8,128)(2,1)S(1)} %all_gather.57) | copy-start | bytes 884740
  142.9 41.0 %copy-start.17 = (bf16[768,192]{1,0:T(8,128)(2,1)}, bf16[768,192]{1,0:T(8,128)(2,1)S(1)}, u32[]{:S(2)}) copy-start(bf16[768,192]{1,0:T(8,128)(2,1)S(1)} %all_gather.59) | copy-start | bytes 884740
  174.1 9.8 copy-start.19
  174.1 6.3 copy-start.15
  417.1 6.8 copy-start.13
  424.0 135.2 %all-gather.12.cloned.1.call-start = ((), (), s32[]{:S(2)}) async-start(), calls=%async_computation.13 | async-start | bytes 1327104 | tf_op jit(solution)/shard_map/all_gather | solution.py:152
  424.6 150.6 %all-gather.10.cloned.1.call-start = ((), (), s32[]{:S(2)}) async-start(), calls=%async_computation.12 | async-start | bytes 7864320 | tf_op jit(solution)/shard_map/all_gather | solution.py:194
  528.9 96.1 %all-gather.14.cloned.1.call-start = ((), (), s32[]{:S(2)}) async-start(), calls=%async_computation.14 | async-start | bytes 1327104 | tf_op jit(solution)/shard_map/all_gather | solution.py:153
  529.5 205.6 %reduce-scatter.24.cloned.1.call-start = ((), (), s32[]{:S(2)}) async-start(), calls=%async_computation.15 | async-start | bytes 15728640 | tf_op jit(solution)/shard_map/reduce_scatter | solution.py:205
  575.2 17.9 %copy-start.32 = (f32[768]{0:T(1024)S(1)}, f32[768]{0:T(1024)}, u32[]{:S(2)}) copy-start(f32[768]{0:T(1024)} %reshape.287) | copy-start | bytes 9220
  588.7 4.5 copy-start.8
  635.2 302.5 %reduce-scatter.26.cloned.1.call-start = ((), (), s32[]{:S(2)}) async-start(), calls=%async_computation.16 | async-start | bytes 15728640 | tf_op jit(solution)/shard_map/reduce_scatter | solution.py:244
  747.4 36.3 %collective-permute-start = (bf16[2,512,768]{2,1,0:T(8,128)(2,1)}, bf16[2,512,768]{2,1,0:T(8,128)(2,1)}, u32[]{:S(2)}, u32[]{:S(2)}) collective-permute-start(bf16[2,512,768]{2,1,0:T(8,128)(2,1)} %get-tuple-element.835), channel_id=1, source_target_pairs={{0,1},{1,2},{2,3},{3,0},{4,5},{5,6},{6,7},{7,4},{8,9},{9,10},{10,1... | collective-permute-start | bytes 4718600 | tf_op jit(solution)/shard_map/ppermute | solution.py:219
  747.4 46.3 %collective-permute-start.1 = (bf16[2,512,768]{2,1,0:T(8,128)(2,1)}, bf16[2,512,768]{2,1,0:T(8,128)(2,1)}, u32[]{:S(2)}, u32[]{:S(2)}) collective-permute-start(bf16[2,512,768]{2,1,0:T(8,128)(2,1)} %get-tuple-element.835), channel_id=1, source_target_pairs={{0,3},{1,0},{2,1},{3,2},{4,7},{5,4},{6,5},{7,6},{8,11},{9,8},{10,9... | collective-permute-start | bytes 4718600 | tf_op jit(solution)/shard_map/ppermute | solution.py:224
  783.8 20.2 %collective-permute-start.2 = (bf16[2,512,768]{2,1,0:T(8,128)(2,1)}, bf16[2,512,768]{2,1,0:T(8,128)(2,1)}, u32[]{:S(2)}, u32[]{:S(2)}) collective-permute-start(bf16[2,512,768]{2,1,0:T(8,128)(2,1)} %collective-permute-done), channel_id=1, source_target_pairs={{0,1},{1,2},{2,3},{3,0},{4,5},{5,6},{6,7},{7,4},{8,9},{9,10},{10,1... | collective-permute-start | bytes 4718600 | tf_op jit(solution)/shard_map/ppermute | solution.py:219
  809.3 18.0 %copy-start.39 = (bf16[768,768]{1,0:T(8,128)(2,1)S(1)}, bf16[768,768]{1,0:T(8,128)(2,1)}, u32[]{:S(2)}) copy-start(bf16[768,768]{1,0:T(8,128)(2,1)} %all-gather.12.cloned.1.call-done) | copy-start | bytes 3538948
  837.9 155.4 %all-gather.16.cloned.1.call-start = ((), (), s32[]{:S(2)}) async-start(), calls=%async_computation.17 | async-start | bytes 7864320 | tf_op jit(solution)/shard_map/all_gather | solution.py:250
  937.7 4.3 copy-start.29
  943.2 50.1 %copy-start.14 = (bf16[2,2048,192]{1,0,2:T(2,128)(2,1)S(1)}, bf16[2,2048,192]{1,0,2:T(2,128)(2,1)}, u32[]{:S(2)}) copy-start(bf16[2,2048,192]{1,0,2:T(2,128)(2,1)} %copy-done.13) | copy-start | bytes 4718596
  943.2 56.5 %copy-start.25 = (f32[2,512]{1,0:T(2,128)}, f32[2,512]{1,0:T(2,128)S(1)}, u32[]{:S(2)}) copy-start(f32[2,512]{1,0:T(2,128)S(1)} %negate_multiply_fusion.1) | copy-start | bytes 12292
  947.0 551.8 %reduce-scatter.40.cloned.1.call-start = ((), (), s32[]{:S(2)}) async-start(), calls=%async_computation.24 | async-start | bytes 884736
  999.8 500.7 %reduce-scatter.28.cloned.1.call-start = ((), (), s32[]{:S(2)}) async-start(), calls=%async_computation.18 | async-start | bytes 7864320 | tf_op jit(solution)/shard_map/reduce_scatter | solution.py:291
  1006.5 331.4 %copy-start.18 = (bf16[768,192]{1,0:T(8,128)(2,1)S(1)}, bf16[768,192]{1,0:T(8,128)(2,1)}, u32[]{:S(2)}) copy-start(bf16[768,192]{1,0:T(8,128)(2,1)} %copy-done.17) | copy-start | bytes 884740
  1013.9 7.9 copy-start.2
  1039.8 5.8 copy-start
  1049.2 7.9 copy-start.2
  1075.7 5.8 copy-start
  1085.7 7.9 copy-start.2
  1112.2 5.8 copy-start
  1122.1 7.8 copy-start.2
  1148.6 5.8 copy-start
  1158.5 7.2 copy-start.4
  1158.5 7.2 copy-start.10
  1176.6 7.9 copy-start.2
  1202.6 5.8 copy-start
  1211.9 7.9 copy-start.2
  1238.4 5.8 copy-start
  1248.4 7.9 copy-start.2
  1274.9 5.8 copy-start
  1284.8 7.8 copy-start.2
  1311.3 5.8 copy-start
  1321.2 7.1 copy-start.4
  1321.2 7.1 copy-start.10
  1332.2 5.6 copy-start.21
  1337.8 6.4 copy-start.24
  1344.3 6.4 copy-start.12
  1344.3 6.4 copy-start.20
  1362.7 141.2 %reduce-scatter.30.cloned.1.call-start = ((), (), s32[]{:S(2)}) async-start(), calls=%async_computation.19 | async-start | bytes 2654208 | tf_op jit(solution)/shard_map/reduce_scatter | solution.py:301
  1372.9 196.3 %reduce-scatter.32.cloned.1.call-start = ((), (), s32[]{:S(2)}) async-start(), calls=%async_computation.20 | async-start | bytes 2654208 | tf_op jit(solution)/shard_map/reduce_scatter | solution.py:302
  1385.4 250.3 %reduce-scatter.34.cloned.1.call-start = ((), (), s32[]{:S(2)}) async-start(), calls=%async_computation.21 | async-start | bytes 884736
  1392.7 6.1 copy-start.46
  1392.7 7.3 copy-start.38
  1392.7 7.4 copy-start.30
  1392.7 7.4 copy-start.31
  1392.7 7.4 copy-start.34
  1392.8 7.3 copy-start.35
  1392.8 7.3 copy-start.36
  1392.8 7.3 copy-start.37
  1392.8 308.9 %reduce-scatter.36.cloned.1.call-start = ((), (), s32[]{:S(2)}) async-start(), calls=%async_computation.22 | async-start | bytes 884736
  1398.7 369.3 %reduce-scatter.38.cloned.1.call-start = ((), (), s32[]{:S(2)}) async-start(), calls=%async_computation.23 | async-start | bytes 884736
  1450.1 50.4 %copy-start.6 = (f32[2,512,768]{2,1,0:T(8,128)S(1)}, f32[2,512,768]{2,1,0:T(8,128)}, u32[]{:S(2)}) copy-start(f32[2,512,768]{2,1,0:T(8,128)} %copy-done.5) | copy-start | bytes 9437188
  1450.1 50.4 %copy-start.26 = (f32[2,512]{1,0:T(2,128)S(1)}, f32[2,512]{1,0:T(2,128)}, u32[]{:S(2)}) copy-start(f32[2,512]{1,0:T(2,128)} %copy-done.25) | copy-start | bytes 12292
  (32 other events, 86.3 us)
Sparse Core Ops, SparseCore 0:
  10.4 49.0 all-gather.7
  424.1 99.0 reduce-scatter.21
  838.0 99.6 reduce-scatter.25
Sparse Core Ops, SparseCore 1:
  426.7 40.1 all-gather.11
  529.0 46.2 all-gather.9
  577.3 41.4 all-gather.13
  635.3 99.7 reduce-scatter.23
  947.1 46.2 all-gather.15
  999.8 63.3 reduce-scatter.39
  1362.8 59.4 reduce-scatter.27
  1426.3 69.8 reduce-scatter.29
  1500.1 69.1 reduce-scatter.31
  1573.1 62.5 reduce-scatter.33
  1639.4 62.3 reduce-scatter.35
  1705.6 62.3 reduce-scatter.37
